TPU v7x, 256 devices: a whole 4x4x8 slice. The times are simulated.
256 devices in a mesh: seq: 16 (over z, core), head: 16 (over y, x).
Axes of the slice: x: 4, y: 4, z: 8, core: 2. Of those that a mesh axis runs over, the one named last changes fastest.
Arguments:
- queries: bfloat16 [6144, 16384], P('seq', 'head'), may hold values from -5 to 5
- keys: bfloat16 [6144, 1024], P('seq', 'head'), may hold values from -5 to 5
- values: bfloat16 [6144, 1024], P('seq', 'head'), may hold values from -6 to 6
- feat_q: bfloat16 [128, 128, 128], P('head'), may hold values from -0.5 to 0.5
- feat_k: bfloat16 [128, 128, 128], P('head'), may hold values from -0.5 to 0.5
Outputs:
- grad_feat_q: float32 [128, 128, 128], P('head')
- grad_feat_k: float32 [128, 128, 128], P('head')
All inputs are finite; a program needn't handle non-finite values.
Results may differ from a plain program's by a relative error of at most 0.02.
Values may be sent and summed in bfloat16 or wider, within the bound.
A program may use at most 128 MiB of HBM per device.

v0:
```python
import math
import jax
import jax.numpy as jnp
from jax import lax
from jax.sharding import PartitionSpec as P

HIGHEST_MODE = lax.Precision.HIGHEST
MASKED_SCORE = -1e30


def from_partner(block, axis, stride):
    count = lax.axis_size(axis)
    route = []
    for low in range(count):
        high = low | 1 << stride
        if high != low and high < count:
            route += [(low, high), (high, low)]
    return lax.ppermute(block, axis, route)


def in_one_piece(arrays, axis, dim, along):
    columns = [a.reshape(*a.shape[:along], -1) for a in arrays]
    both = jnp.concatenate(columns, axis=along)
    filled, at, done = (lax.all_gather(both, axis, axis=dim, tiled=True), 0, [])
    for a, column in zip(arrays, columns):
        piece = filled[..., at : at + column.shape[along]]
        done.append(piece.reshape(*piece.shape[:along], *a.shape[along:]))
        at += column.shape[along]
    return tuple(done)


def together(arrays, axis):
    vector, at, done = (jnp.concatenate([a.reshape(-1) for a in arrays]), 0, [])
    so_far = lax.psum(vector, axis)
    for a in arrays:
        done.append(so_far[at : at + a.size].reshape(a.shape))
        at += a.size
    return tuple(done)


def split_wide(entries):
    high = entries.astype(jnp.bfloat16)
    low = (entries - high.astype(jnp.float32)).astype(jnp.bfloat16)
    return (high, low)


def wide_left(form, wide, narrow):
    high, low = split_wide(wide)
    return jnp.einsum(form, high, narrow, preferred_element_type=jnp.float32) + jnp.einsum(
        form, low, narrow, preferred_element_type=jnp.float32
    )


def wide_right(form, narrow, wide):
    high, low = split_wide(wide)
    return jnp.einsum(form, narrow, high, preferred_element_type=jnp.float32) + jnp.einsum(
        form, narrow, low, preferred_element_type=jnp.float32
    )


def attend_block(
    running, query_half, query_pos, key_rows, value_rows, key_first, group_count, score_scale
):
    row_peak, row_total, summed = running
    half_rows = query_half.shape[0]
    key_count = key_rows.shape[0]
    head_dim = key_rows.shape[1] // group_count
    grouped = query_half.reshape(half_rows, group_count, -1, head_dim)
    key_heads = key_rows.reshape(key_count, group_count, head_dim)
    value_heads = value_rows.reshape(key_count, group_count, head_dim)
    scores = (
        jnp.einsum("rgjd,kgd->gjrk", grouped, key_heads, preferred_element_type=jnp.float32)
        * score_scale
    )
    scores = scores.reshape(row_peak.shape[0], half_rows, key_count)
    key_pos = key_first + jnp.arange(key_count, dtype=jnp.int32)
    allowed = (key_pos[None, :] <= query_pos[:, None])[None]
    new_peak = jnp.maximum(row_peak, jnp.max(jnp.where(allowed, scores, MASKED_SCORE), axis=-1))
    weights = jnp.exp(jnp.where(allowed, scores - new_peak[..., None], MASKED_SCORE))
    factor = jnp.exp(row_peak - new_peak)
    row_total = row_total * factor + jnp.sum(weights, axis=-1)
    rounded = weights.astype(jnp.bfloat16).reshape(group_count, -1, half_rows, key_count)
    mixture = jnp.einsum("gjrk,kgd->gjrd", rounded, value_heads, preferred_element_type=jnp.float32)
    summed = summed * factor[..., None] + mixture.reshape(summed.shape)
    return (new_peak, row_total, summed)


def body(queries, keys, values, feat_q, feat_k):
    row_count = queries.shape[0]
    heads_here = feat_q.shape[0]
    head_dim = feat_q.shape[1]
    seq_count = lax.axis_size("seq")
    seq_place = lax.axis_index("seq")
    head_place = lax.axis_index("head")
    key_value = jnp.stack((keys, values))
    partner = from_partner(key_value, "head", 0)
    upper_half = head_place // (1 << 0) % 2 == 1
    key_value = jnp.where(
        upper_half,
        jnp.concatenate((partner, key_value), axis=2),
        jnp.concatenate((key_value, partner), axis=2),
    )
    group_count = key_value.shape[2] // head_dim
    group_size = heads_here // group_count
    query_pos = seq_place * row_count + jnp.arange(row_count, dtype=jnp.int32)
    half_rows = row_count // 2
    query_halves = (queries[:half_rows], queries[half_rows:])
    pos_halves = (query_pos[:half_rows], query_pos[half_rows:])
    top_halves = (jnp.max(pos_halves[0]), jnp.max(pos_halves[1]))
    score_scale = head_dim ** (-0.5)
    start_half = (
        jnp.full((heads_here, half_rows), MASKED_SCORE, jnp.float32),
        jnp.zeros((heads_here, half_rows), jnp.float32),
        jnp.zeros((heads_here, half_rows, head_dim), jnp.float32),
    )
    shard_part = lax.all_gather(key_value, "seq", axis=1, tiled=True)
    part_rows = shard_part.shape[1]
    block_rows = math.gcd(part_rows, 512)

    def one_step(step_index, halves_state):
        offset = step_index * block_rows
        key_rows = lax.dynamic_slice_in_dim(shard_part[0], offset, block_rows, 0)
        value_rows = lax.dynamic_slice_in_dim(shard_part[1], offset, block_rows, 0)
        updated = []
        for half_index in range(2):

            def attend_half(current, half_index=half_index):
                return attend_block(
                    current,
                    query_halves[half_index],
                    pos_halves[half_index],
                    key_rows,
                    value_rows,
                    offset,
                    group_count,
                    score_scale,
                )

            def unchanged(current):
                return current

            updated.append(
                lax.cond(
                    top_halves[half_index] >= offset,
                    attend_half,
                    unchanged,
                    halves_state[half_index],
                )
            )
        return tuple(updated)

    finished = lax.fori_loop(0, part_rows // block_rows, one_step, (start_half, start_half))
    teacher_out = jnp.concatenate(
        [
            (finished[half_index][2] / finished[half_index][1][..., None]).astype(jnp.bfloat16)
            for half_index in range(2)
        ],
        axis=1,
    )
    key_local = key_value[0].reshape(row_count, group_count, head_dim)
    value_local = key_value[1].reshape(row_count, group_count, head_dim)
    query_local = queries.reshape(row_count, heads_here, head_dim)
    query_pre = jnp.einsum("rhd,hdf->hrf", query_local, feat_q, preferred_element_type=jnp.float32)
    key_pre = jnp.einsum(
        "rgd,gjdf->gjrf",
        key_local,
        feat_k.reshape(group_count, group_size, head_dim, -1),
        preferred_element_type=jnp.float32,
    ).reshape(heads_here, row_count, -1)
    feat_count = query_pre.shape[-1]
    query_feat = jax.nn.softplus(query_pre).astype(jnp.bfloat16)
    key_feat = jax.nn.softplus(key_pre).astype(jnp.bfloat16)
    block_state = jnp.einsum(
        "gjrf,rgd->gjfd",
        key_feat.reshape(group_count, group_size, row_count, -1),
        value_local,
        preferred_element_type=jnp.float32,
    ).reshape(heads_here, feat_count, head_dim)
    block_norm = jnp.sum(key_feat, axis=1, dtype=jnp.float32)
    zero_pair = (jnp.zeros_like(block_state), jnp.zeros_like(block_norm))
    take_shard_part = tuple(
        (
            part.astype(jnp.float32)
            for part in in_one_piece(
                (block_state[None].astype(jnp.bfloat16), block_norm[None].astype(jnp.bfloat16)),
                "seq",
                0,
                3,
            )
        )
    )
    part_count = take_shard_part[0].shape[0]
    chosen = jnp.arange(part_count, dtype=jnp.int32) < seq_place
    before_state = zero_pair[0] + jnp.sum(
        jnp.where(chosen[:, None, None, None], take_shard_part[0], 0.0), axis=0
    )
    before_norm = zero_pair[1] + jnp.sum(
        jnp.where(chosen[:, None, None], take_shard_part[1], 0.0), axis=0
    )
    causal = jnp.arange(row_count)[:, None] >= jnp.arange(row_count)[None, :]
    affinity = jnp.einsum("hrf,hsf->hrs", query_feat, key_feat, preferred_element_type=jnp.float32)
    masked = jnp.where(causal[None], affinity, 0.0)
    local_mix = jnp.einsum(
        "gjrs,sgd->gjrd",
        masked.astype(jnp.bfloat16).reshape(group_count, group_size, row_count, row_count),
        value_local,
        preferred_element_type=jnp.float32,
    ).reshape(heads_here, row_count, head_dim)
    numerator = wide_right("hrf,hfd->hrd", query_feat, before_state) + local_mix
    denominator = wide_right("hrf,hf->hr", query_feat, before_norm) + jnp.sum(masked, axis=-1)
    student = numerator / denominator[..., None]
    total_tokens = row_count * seq_count
    grad_out = 2.0 * (student - teacher_out.astype(jnp.float32)) / total_tokens
    grad_numer = grad_out / denominator[..., None]
    grad_denom = -jnp.sum(grad_out * student, axis=-1) / denominator
    back_state = wide_right("hrf,hrd->hfd", query_feat, grad_numer)
    back_norm = wide_right("hrf,hr->hf", query_feat, grad_denom)

    def take_upper(running, shard_part):
        part_count = shard_part[0].shape[0]
        chosen = jnp.arange(part_count, dtype=jnp.int32) > seq_place
        return (
            running[0]
            + jnp.sum(jnp.where(chosen[:, None, None, None], shard_part[0], 0.0), axis=0),
            running[1] + jnp.sum(jnp.where(chosen[:, None, None], shard_part[1], 0.0), axis=0),
        )

    after_state, after_norm = take_upper(
        zero_pair,
        (
            lax.all_gather(back_state[None].astype(jnp.bfloat16), "seq", axis=0, tiled=True).astype(
                jnp.float32
            ),
            lax.all_gather(back_norm[None].astype(jnp.bfloat16), "seq", axis=0, tiled=True).astype(
                jnp.float32
            ),
        ),
    )
    grad_aff = wide_left(
        "gjrd,sgd->gjrs",
        grad_numer.reshape(group_count, group_size, row_count, head_dim),
        value_local,
    ).reshape(heads_here, row_count, row_count)
    grad_aff = jnp.where(causal[None], grad_aff + grad_denom[..., None], 0.0)
    grad_qfeat = (
        jnp.einsum("hrd,hfd->hrf", grad_numer, before_state, precision=HIGHEST_MODE)
        + grad_denom[..., None] * before_norm[:, None, :]
        + wide_left("hrs,hsf->hrf", grad_aff, key_feat)
    )
    grad_kfeat = (
        wide_right(
            "sgd,gjfd->gjsf",
            value_local,
            after_state.reshape(group_count, group_size, feat_count, head_dim),
        ).reshape(heads_here, row_count, feat_count)
        + after_norm[:, None, :]
        + wide_left("hrs,hrf->hsf", grad_aff, query_feat)
    )
    grad_wq = wide_right("rhd,hrf->hdf", query_local, grad_qfeat * jax.nn.sigmoid(query_pre))
    grad_wk = wide_right(
        "rgd,gjrf->gjdf",
        key_local,
        (grad_kfeat * jax.nn.sigmoid(key_pre)).reshape(
            group_count, group_size, row_count, feat_count
        ),
    ).reshape(heads_here, head_dim, feat_count)
    return tuple(
        (
            part.astype(jnp.float32)
            for part in together(
                (grad_wq.astype(jnp.bfloat16), grad_wk.astype(jnp.bfloat16)), "seq"
            )
        )
    )


def solution(mesh):
    return jax.shard_map(
        body,
        mesh=mesh,
        in_specs=(
            P("seq", "head"),
            P("seq", "head"),
            P("seq", "head"),
            P("head", None, None),
            P("head", None, None),
        ),
        out_specs=(P("head", None, None), P("head", None, None)),
        check_vma=False,
    )
```

profile of v0, /device:TPU:1, one launch (start us, length us, event | category | flops | bytes accessed | tf_op | source)
XLA Modules:
  0.0 392.3 jit_solution(10411164082974506304)
XLA Ops:
  9.3 2.1 collective-permute-start
  11.4 3.4 collective-permute-done
  21.4 2.2 select_reduce_fusion.1
  23.7 38.1 %all-gather.8.cloned.1.call-done = bf16[2,6144,128]{2,1,0:T(8,128)(2,1)} async-done(((bf16[2,384,128]{2,1,0:T(8,128)(2,1)}), bf16[2,6144,128]{2,1,0:T(8,128)(2,1)}) %all-gather.8.cloned.1.call-update) | async-done | bytes 3145744 | tf_op jit(solution)/shard_map/all_gather | solution.py:116
  62.8 56.6 %while.23 = (s32[]{:T(128)}, f32[8,192]{1,0:T(8,128)S(1)}, f32[8,192]{1,0:T(8,128)S(1)}, f32[8,192,128]{2,1,0:T(8,128)}, f32[8,192]{1,0:T(8,128)S(1)}, /*index=5...) while((s32[]{:T(128)}, f32[8,192]{1,0:T(8,128)S(1)}, ...), condition=%wide.region_15.16_spmd, body=%wide.region_6.15_spmd.sunk | while | flops 823598080 | bytes 37431328 | solution.py:152
  66.2 4.4 %conditional.4 = ((f32[8,192]{1,0:T(8,128)S(1)}, f32[8,192]{1,0:T(8,128)S(1)}, f32[8,192,128]{2,1,0:T(8,128)})) conditional(s32[]{:T(128)} %convert_element_type.400, (f32[8,192]{1,0:T(8,128)S(1)}, f32[8,192]{1,0:T(8,128)S(1)}, f32[8,192,128]{2,1,0:T(8,128)}) %tuple.74, (s32[]{:T(128)}, s32[192]{0:T(256)S(1)}, bf16[192,1024]{1,0:T(8,128)(2,1)S(1)}, ...), branch_computations={%region_7.7_spmd, %region_8.10_spmd} | conditional | flops 411799040 | bytes 18453340 | solution.py:143
  70.6 3.5 conditional.5
  77.4 4.4 %conditional.4 = ((f32[8,192]{1,0:T(8,128)S(1)}, f32[8,192]{1,0:T(8,128)S(1)}, f32[8,192,128]{2,1,0:T(8,128)})) conditional(s32[]{:T(128)} %convert_element_type.400, (f32[8,192]{1,0:T(8,128)S(1)}, f32[8,192]{1,0:T(8,128)S(1)}, f32[8,192,128]{2,1,0:T(8,128)}) %tuple.74, (s32[]{:T(128)}, s32[192]{0:T(256)S(1)}, bf16[192,1024]{1,0:T(8,128)(2,1)S(1)}, ...), branch_computations={%region_7.7_spmd, %region_8.10_spmd} | conditional | flops 411799040 | bytes 18453340 | solution.py:143
  81.9 3.5 conditional.5
  86.6 2.1 fusion.153
  90.0 2.2 fusion.153
  93.5 2.1 fusion.153
  96.9 2.1 fusion.153
  121.8 2.5 copy.124
  124.3 2.4 divide_convert_fusion
  126.7 4.6 %slice.72 = bf16[16,8,128,128]{2,1,3,0:T(8,128)(2,1)} slice(bf16[16,8,128,129]{2,1,3,0:T(8,128)(2,1)} %all-gather.6.cloned.1.call-done), slice={[0:16], [0:8], [0:128], [0:128]} | slice | bytes 8388608 | tf_op jit(solution)/shard_map/slice | solution.py:26
  131.2 6.7 %copy.186 = bf16[16,8,128,128]{3,2,1,0:T(8,128)(2,1)} copy(bf16[16,8,128,128]{2,1,3,0:T(8,128)(2,1)} %slice.72) | data formatting | bytes 8388608
  137.9 3.2 select_reduce_fusion
  147.3 2.8 fusion.128
  158.5 91.9 %all-gather.1 = bf16[128,128]{1,0:T(8,128)(2,1)S(1)} all-gather(bf16[8,128]{1,0:T(8,128)(2,1)S(1)} %add_convert_fusion), channel_id=3, replica_groups=mesh['seq'=16,'head'=16] {'seq'}, dimensions={0}, use_global_device_ids=true | all-gather | bytes 34816 | tf_op jit(solution)/shard_map/all_gather | solution.py:234
  250.5 4.7 %fusion.117 = f32[8,384,128]{2,1,0:T(8,128)S(1)} fusion(bf16[8,384,128]{2,1,0:T(8,128)(2,1)S(1)} %select_convert_fusion.2, f32[8,384,384]{1,2,0:T(8,128)} %copy-done.2), kind=kOutput, calls=%fused_computation.179 | convolution fusion | flops 306708480 | bytes 7077888 | tf_op jit(solution)/shard_map/hrs,hrf->hsf/dot_general | solution.py:49
  257.2 7.9 %all-gather.10.cloned.1.call-done = bf16[128,128,128]{2,1,0:T(8,128)(2,1)} async-done(((bf16[8,128,128]{2,1,0:T(8,128)(2,1)}), bf16[128,128,128]{2,1,0:T(8,128)(2,1)}) %all-gather.10.cloned.1.call-update) | async-done | bytes 4194320 | tf_op jit(solution)/shard_map/all_gather | solution.py:231
  265.1 3.2 fusion.48
  274.2 108.8 %all-reduce.2.cloned.1.call-done = bf16[262144]{0:T(1024)(128)(2,1)} async-done(((bf16[262144]{0:T(1024)(128)(2,1)}), bf16[262144]{0:T(1024)(128)(2,1)}) %all-reduce.2.cloned.1.call-update) | async-done | bytes 524304 | tf_op jit(solution)/shard_map/psum | solution.py:34
  (189 shorter events, 70.1 us)
Async XLA Ops:
  7.2 10.8 %copy-start = (bf16[8,128,128]{2,1,0:T(8,128)(2,1)S(1)}, bf16[8,128,128]{2,1,0:T(8,128)(2,1)}, u32[]{:S(2)}) copy-start(bf16[8,128,128]{2,1,0:T(8,128)(2,1)} %param.15) | copy-start | bytes 786436
  7.2 9.3 %copy-start.5 = (bf16[384,1024]{1,0:T(8,128)(2,1)S(1)}, bf16[384,1024]{1,0:T(8,128)(2,1)}, u32[]{:S(2)}) copy-start(bf16[384,1024]{1,0:T(8,128)(2,1)} %param.11) | copy-start | bytes 2359300
  7.2 54.6 %all-gather.8.cloned.1.call-start = ((), (), s32[]{:S(2)}) async-start(), calls=%async_computation.1 | async-start | bytes 3342336 | tf_op jit(solution)/shard_map/all_gather | solution.py:116
  8.2 8.3 %copy-start.18 = (bf16[8,128,128]{2,1,0:T(8,128)(2,1)S(1)}, bf16[8,128,128]{2,1,0:T(8,128)(2,1)}, u32[]{:S(2)}) copy-start(bf16[8,128,128]{2,1,0:T(8,128)(2,1)} %param.14) | copy-start | bytes 786436
  9.3 5.5 %collective-permute-start = (bf16[2,384,64]{2,1,0:T(8,128)(2,1)S(1)}, bf16[2,384,64]{2,1,0:T(8,128)(2,1)S(1)}, u32[]{:S(2)}, u32[]{:S(2)}) collective-permute-start(bf16[2,384,64]{2,1,0:T(8,128)(2,1)S(1)} %pad_maximum_fusion.3), channel_id=1, source_target_pairs={{0,1},{1,0},{2,3},{3,2},{4,5},{5,4},{6,7},{7,6},{8,9},{9,8},{10,11... | collective-permute-start | bytes 294920 | tf_op jit(solution)/shard_map/ppermute | solution.py:18
  15.7 111.0 %all-gather.6.cloned.1.call-start = ((), (), s32[]{:S(2)}) async-start(), calls=%async_computation | async-start | bytes 4491264 | tf_op jit(solution)/shard_map/all_gather | solution.py:24
  17.0 2.2 copy-start.3
  17.0 1.1 copy-start.8
  19.2 1.2 copy-start.14
  19.2 2.2 copy-start.9
  21.2 243.9 %all-gather.10.cloned.1.call-start = ((), (), s32[]{:S(2)}) async-start(), calls=%async_computation.3 | async-start | bytes 4456448 | tf_op jit(solution)/shard_map/all_gather | solution.py:231
  67.1 1.1 copy-start.12
  78.4 1.2 copy-start.12
  141.8 2.4 copy-start.19
  142.2 1.9 copy-start.16
  142.3 1.9 copy-start.17
  147.0 236.0 %all-reduce.2.cloned.1.call-start = ((), (), s32[]{:S(2)}) async-start(), calls=%async_computation.2 | async-start | bytes 1048576 | tf_op jit(solution)/shard_map/psum | solution.py:34
  152.0 2.1 copy-start.2
  152.0 2.5 copy-start.4
  154.5 1.7 copy-start.6
  156.2 99.0 %slice-start = ((s8[4718592]{0:T(1024)(128)(4,1)}), s8[524288]{0:T(1024)(128)(4,1)S(1)}, s32[]{:S(2)}) async-start(s8[4718592]{0:T(1024)(128)(4,1)} %bitcast.271), calls=%async_computation.4 | async-start | bytes 1048576
  158.2 97.0 %slice-start.1 = ((s8[4718592]{0:T(1024)(128)(4,1)}), s8[4194304]{0:T(1024)(128)(4,1)S(1)}, s32[]{:S(2)}) async-start(s8[4718592]{0:T(1024)(128)(4,1)} %bitcast.271), calls=%async_computation.5 | async-start | bytes 8388608
  268.5 1.4 copy-start.7
  274.2 111.6 %copy-start.1 = (bf16[8,128,128]{2,1,0:T(8,128)(2,1)S(1)}, bf16[8,128,128]{2,1,0:T(8,128)(2,1)}, u32[]{:S(2)}) copy-start(bf16[8,128,128]{2,1,0:T(8,128)(2,1)} %param.15) | copy-start | bytes 786436
  (5 other events, 4.8 us)
Sparse Core Ops, SparseCore 0:
  15.8 45.9 all-gather.7
  63.7 40.6 all-gather.5
  147.1 117.8 all-gather.9
  274.3 108.6 all-reduce.1
where the time goes:
time: 394 us; the launch traced here: 392 us
  waiting for transfers between devices  158 us (40%)
  blocking collectives  91.9 us (23%)
  local copies, waits for them, and re-layouts  53.3 us (14%)
  matrix products  36.4 us (9%)
  other arithmetic  20.1 us (5%)
  loops' own time  15.4 us (4%)
  between operations  14.2 us (4%)
    psum x1, waiting for transfers between devices, together(): so_far = lax.psum(vector, axis)  109 us
    all_gather x1, blocking collectives, body(): lax.all_gather(back_norm[None].astype(jnp.bfloat16), 'seq', axis=0, tiled...  91.9 us
    all_gather x1, waiting for transfers between devices, body(): shard_part = lax.all_gather(key_value, 'seq', axis=1, tiled=True)  38.1 us
    slice x12, local copies, waits for them, and re-layouts, one_step(): value_rows = lax.dynamic_slice_in_dim(shard_part[1], offset, block_rows, 0)  25.2 us
    another operation x1, loops' own time, body(): lax.fori_loop(0, part_rows // block_rows, one_step, (start_half, start_ha...  14.8 us
    unnamed x45, local copies, waits for them, and re-layouts  13.5 us
  transfers between devices with their start and end apart: 5, of which 4 were waited for; matrix products, arithmetic and copies ran while one was open for 18% of the time, Pallas kernels for 0%

commit v1 on v0

--- a/solution.py
+++ b/solution.py
@@ -225,15 +225,22 @@
             running[1] + jnp.sum(jnp.where(chosen[:, None, None], shard_part[1], 0.0), axis=0),
         )
 
+    supply_slabs_up = lambda vec: jnp.concatenate(
+        lax.all_to_all(
+            jnp.stack([vec for _ in range(lax.axis_size("seq"))]),
+            "seq",
+            split_axis=0,
+            concat_axis=0,
+        ),
+        axis=0,
+    )
     after_state, after_norm = take_upper(
         zero_pair,
         (
             lax.all_gather(back_state[None].astype(jnp.bfloat16), "seq", axis=0, tiled=True).astype(
                 jnp.float32
             ),
-            lax.all_gather(back_norm[None].astype(jnp.bfloat16), "seq", axis=0, tiled=True).astype(
-                jnp.float32
-            ),
+            supply_slabs_up(back_norm[None].astype(jnp.bfloat16)).astype(jnp.float32),
         ),
     )
     grad_aff = wide_left(

time: 394 us -> 411 us (1.043)
  starting transfers between devices: 2.68 us -> 98.3 us
  blocking collectives: 91.9 us -> 0 us
  waiting for transfers between devices: 158 us -> 171 us
    all_to_all x0 -> x1, starting transfers between devices: none -> 95.9 us  [body(): lax.all_to_all(jnp.stack([vec for _ in range(lax.axis_size('seq'))]), 'se...]
    all_gather x1 -> x0, blocking collectives: 91.9 us -> none  [body(): lax.all_gather(back_norm[None].astype(jnp.bfloat16), 'seq', axis=0, tiled...]
    all_gather x1, waiting for transfers between devices: 7.88 us -> 22 us  [body(): lax.all_gather(back_state[None].astype(jnp.bfloat16), 'seq', axis=0, tile...]
    unnamed x45 -> x53, local copies, waits for them, and re-layouts: 13.5 us -> 12.2 us
  transfers between devices with their start and end apart: 5 -> 6, of which waited for: 4 -> 4; matrix products, arithmetic and copies ran while one was open for 18% -> 18% of each run, Pallas kernels for 0% -> 0%
where the time goes in v1:
time: 411 us; the launch traced here: 409 us
  waiting for transfers between devices  171 us (42%)
  starting transfers between devices  98.3 us (24%)
  local copies, waits for them, and re-layouts  52 us (13%)
  matrix products  34.2 us (8%)
  other arithmetic  24 us (6%)
  loops' own time  15.5 us (4%)
  between operations  14.3 us (3%)
    psum x1, waiting for transfers between devices, together(): so_far = lax.psum(vector, axis)  109 us
    all_to_all x1, starting transfers between devices, body(): lax.all_to_all(jnp.stack([vec for _ in range(lax.axis_size('seq'))]), 'se...  95.9 us
    all_gather x1, waiting for transfers between devices, body(): shard_part = lax.all_gather(key_value, 'seq', axis=1, tiled=True)  36.4 us
    slice x12, local copies, waits for them, and re-layouts, one_step(): value_rows = lax.dynamic_slice_in_dim(shard_part[1], offset, block_rows, 0)  25.2 us
    all_gather x1, waiting for transfers between devices, body(): lax.all_gather(back_state[None].astype(jnp.bfloat16), 'seq', axis=0, tile...  22 us
    another operation x1, loops' own time, body(): lax.fori_loop(0, part_rows // block_rows, one_step, (start_half, start_ha...  14.9 us
    unnamed x53, local copies, waits for them, and re-layouts  12.2 us
  transfers between devices with their start and end apart: 6, of which 4 were waited for; matrix products, arithmetic and copies ran while one was open for 18% of the time, Pallas kernels for 0%

profile of v1, /device:TPU:1, one launch (start us, length us, event | category | flops | bytes accessed | tf_op | source)
XLA Modules:
  0.0 409.2 jit_solution(2829315681010580472)
XLA Ops:
  9.3 2.1 collective-permute-start
  11.4 3.4 collective-permute-done
  22.6 2.8 select_reduce_fusion.1
  25.4 36.4 %all-gather.7.cloned.1.call-done = bf16[2,6144,128]{2,1,0:T(8,128)(2,1)} async-done(((bf16[2,384,128]{2,1,0:T(8,128)(2,1)}), bf16[2,6144,128]{2,1,0:T(8,128)(2,1)}) %all-gather.7.cloned.1.call-update) | async-done | bytes 3145744 | tf_op jit(solution)/shard_map/all_gather | solution.py:116
  62.9 59.4 %while.23 = (s32[]{:T(128)}, f32[8,192]{1,0:T(8,128)S(1)}, f32[8,192]{1,0:T(8,128)S(1)}, f32[8,192,128]{2,1,0:T(8,128)}, f32[8,192]{1,0:T(8,128)S(1)}, /*index=5...) while((s32[]{:T(128)}, f32[8,192]{1,0:T(8,128)S(1)}, ...), condition=%wide.region_15.16_spmd, body=%wide.region_6.15_spmd.sunk | while | flops 823598080 | bytes 37431328 | solution.py:152
  66.2 5.2 %conditional.4 = ((f32[8,192]{1,0:T(8,128)S(1)}, f32[8,192]{1,0:T(8,128)S(1)}, f32[8,192,128]{2,1,0:T(8,128)})) conditional(s32[]{:T(128)} %convert_element_type.401, (f32[8,192]{1,0:T(8,128)S(1)}, f32[8,192]{1,0:T(8,128)S(1)}, f32[8,192,128]{2,1,0:T(8,128)}) %tuple.74, (s32[]{:T(128)}, s32[192]{0:T(256)}, bf16[192,1024]{1,0:T(8,128)(2,1)S(1)}, ...), branch_computations={%region_7.7_spmd, %region_8.10_spmd} | conditional | flops 411799040 | bytes 18453340 | solution.py:143
  71.4 4.2 %conditional.5 = ((f32[8,192]{1,0:T(8,128)S(1)}, f32[8,192]{1,0:T(8,128)S(1)}, f32[8,192,128]{2,1,0:T(8,128)S(1)})) conditional(s32[]{:T(128)} %convert_element_type.402, (f32[8,192]{1,0:T(8,128)S(1)}, f32[8,192]{1,0:T(8,128)S(1)}, f32[8,192,128]{2,1,0:T(8,128)S(1)}) %tuple.76, (s32[]{:T(128)}, s32[192]{0:T(256)}, ...), branch_computations={%region_11.11_spmd, %region_12.14_spmd} | conditional | flops 411799040 | bytes 12161828 | solution.py:143
  76.8 2.1 fusion.153
  78.9 5.2 %conditional.4 = ((f32[8,192]{1,0:T(8,128)S(1)}, f32[8,192]{1,0:T(8,128)S(1)}, f32[8,192,128]{2,1,0:T(8,128)})) conditional(s32[]{:T(128)} %convert_element_type.401, (f32[8,192]{1,0:T(8,128)S(1)}, f32[8,192]{1,0:T(8,128)S(1)}, f32[8,192,128]{2,1,0:T(8,128)}) %tuple.74, (s32[]{:T(128)}, s32[192]{0:T(256)}, bf16[192,1024]{1,0:T(8,128)(2,1)S(1)}, ...), branch_computations={%region_7.7_spmd, %region_8.10_spmd} | conditional | flops 411799040 | bytes 18453340 | solution.py:143
  84.1 4.2 %conditional.5 = ((f32[8,192]{1,0:T(8,128)S(1)}, f32[8,192]{1,0:T(8,128)S(1)}, f32[8,192,128]{2,1,0:T(8,128)S(1)})) conditional(s32[]{:T(128)} %convert_element_type.402, (f32[8,192]{1,0:T(8,128)S(1)}, f32[8,192]{1,0:T(8,128)S(1)}, f32[8,192,128]{2,1,0:T(8,128)S(1)}) %tuple.76, (s32[]{:T(128)}, s32[192]{0:T(256)}, ...), branch_computations={%region_11.11_spmd, %region_12.14_spmd} | conditional | flops 411799040 | bytes 12161828 | solution.py:143
  89.5 2.1 fusion.153
  92.9 2.1 fusion.153
  96.4 2.1 fusion.153
  124.7 2.4 copy.125
  127.1 2.4 divide_convert_fusion
  129.5 4.6 %slice.72 = bf16[16,8,128,128]{2,1,3,0:T(8,128)(2,1)} slice(bf16[16,8,128,129]{2,1,3,0:T(8,128)(2,1)} %all-gather.5.cloned.1.call-done), slice={[0:16], [0:8], [0:128], [0:128]} | slice | bytes 8388608 | tf_op jit(solution)/shard_map/slice | solution.py:26
  134.1 6.8 %copy.188 = bf16[16,8,128,128]{3,2,1,0:T(8,128)(2,1)} copy(bf16[16,8,128,128]{2,1,3,0:T(8,128)(2,1)} %slice.72) | data formatting | bytes 8388608
  140.9 3.2 select_reduce_fusion
  151.4 95.9 %all-to-all-start = ((bf16[16,1,8,128]{3,2,1,0:T(8,128)(2,1)}), bf16[16,1,8,128]{3,2,1,0:T(8,128)(2,1)S(1)}, u32[]{:S(2)}, u32[]{:S(2)}) async-start(bf16[16,1,8,128]{3,2,1,0:T(8,128)(2,1)} %stack.11), calls=%async_computation | async-start | bytes 65536 | tf_op jit(solution)/shard_map/all_to_all | solution.py:229
  247.3 3.8 fusion.128
  260.1 22.0 %all-gather.9.cloned.1.call-done = bf16[128,128,128]{2,1,0:T(8,128)(2,1)} async-done(((bf16[8,128,128]{2,1,0:T(8,128)(2,1)}), bf16[128,128,128]{2,1,0:T(8,128)(2,1)}) %all-gather.9.cloned.1.call-update) | async-done | bytes 4194320 | tf_op jit(solution)/shard_map/all_gather | solution.py:240
  282.1 3.2 fusion.48
  286.9 2.1 fusion.55
  290.9 109.0 %all-reduce.2.cloned.1.call-done = bf16[262144]{0:T(1024)(128)(2,1)} async-done(((bf16[262144]{0:T(1024)(128)(2,1)}), bf16[262144]{0:T(1024)(128)(2,1)}) %all-reduce.2.cloned.1.call-update) | async-done | bytes 524304 | tf_op jit(solution)/shard_map/psum | solution.py:34
  (198 shorter events, 71.2 us)
Async XLA Ops:
  7.2 11.9 %copy-start = (bf16[8,128,128]{2,1,0:T(8,128)(2,1)S(1)}, bf16[8,128,128]{2,1,0:T(8,128)(2,1)}, u32[]{:S(2)}) copy-start(bf16[8,128,128]{2,1,0:T(8,128)(2,1)} %param.15) | copy-start | bytes 786436
  7.2 10.5 %copy-start.4 = (bf16[384,1024]{1,0:T(8,128)(2,1)S(1)}, bf16[384,1024]{1,0:T(8,128)(2,1)}, u32[]{:S(2)}) copy-start(bf16[384,1024]{1,0:T(8,128)(2,1)} %param.11) | copy-start | bytes 2359300
  7.2 54.6 %all-gather.7.cloned.1.call-start = ((), (), s32[]{:S(2)}) async-start(), calls=%async_computation.2 | async-start | bytes 3342336 | tf_op jit(solution)/shard_map/all_gather | solution.py:116
  8.2 9.5 %copy-start.19 = (bf16[8,128,128]{2,1,0:T(8,128)(2,1)S(1)}, bf16[8,128,128]{2,1,0:T(8,128)(2,1)}, u32[]{:S(2)}) copy-start(bf16[8,128,128]{2,1,0:T(8,128)(2,1)} %param.14) | copy-start | bytes 786436
  9.3 5.5 %collective-permute-start = (bf16[2,384,64]{2,1,0:T(8,128)(2,1)S(1)}, bf16[2,384,64]{2,1,0:T(8,128)(2,1)S(1)}, u32[]{:S(2)}, u32[]{:S(2)}) collective-permute-start(bf16[2,384,64]{2,1,0:T(8,128)(2,1)S(1)} %pad_maximum_fusion.3), channel_id=1, source_target_pairs={{0,1},{1,0},{2,3},{3,2},{4,5},{5,4},{6,7},{7,6},{8,9},{9,8},{10,11... | collective-permute-start | bytes 294920 | tf_op jit(solution)/shard_map/ppermute | solution.py:18
  15.7 113.9 %all-gather.5.cloned.1.call-start = ((), (), s32[]{:S(2)}) async-start(), calls=%async_computation.1 | async-start | bytes 4491264 | tf_op jit(solution)/shard_map/all_gather | solution.py:24
  16.3 6.2 %copy-start.15 = (pred[384,384]{0,1:T(8,128)(4,1)}, pred[384,384]{0,1:T(8,128)(4,1)S(1)}, u32[]{:S(2)}) copy-start(pred[384,384]{0,1:T(8,128)(4,1)S(1)} %iota_compare_fusion) | copy-start | bytes 442372
  18.1 2.2 copy-start.2
  20.4 2.2 copy-start.9
  22.3 259.8 %all-gather.9.cloned.1.call-start = ((), (), s32[]{:S(2)}) async-start(), calls=%async_computation.4 | async-start | bytes 4456448 | tf_op jit(solution)/shard_map/all_gather | solution.py:240
  134.1 6.8 %copy-start.23 = (pred[16]{0:T(512)(128)(4,1)S(1)}, pred[16]{0:T(512)(128)(4,1)}, u32[]{:S(2)}) copy-start(pred[16]{0:T(512)(128)(4,1)} %iota_compare_fusion.2) | copy-start | bytes 52
  144.9 2.4 copy-start.22
  144.9 2.4 copy-start.25
  145.4 2.0 copy-start.7
  145.4 2.0 copy-start.16
  145.4 2.0 copy-start.17
  145.4 2.0 copy-start.18
  146.5 2.0 copy-start.20
  150.2 109.8 %copy-start.24 = (pred[16]{0:T(512)(128)(4,1)}, pred[16]{0:T(512)(128)(4,1)S(1)}, u32[]{:S(2)}) copy-start(pred[16]{0:T(512)(128)(4,1)S(1)} %iota_compare_fusion.1) | copy-start | bytes 52
  151.4 108.6 %all-to-all-start = ((bf16[16,1,8,128]{3,2,1,0:T(8,128)(2,1)}), bf16[16,1,8,128]{3,2,1,0:T(8,128)(2,1)S(1)}, u32[]{:S(2)}, u32[]{:S(2)}) async-start(bf16[16,1,8,128]{3,2,1,0:T(8,128)(2,1)} %stack.11), calls=%async_computation | async-start | bytes 65536 | tf_op jit(solution)/shard_map/all_to_all | solution.py:229
  247.3 152.7 %all-reduce.2.cloned.1.call-start = ((), (), s32[]{:S(2)}) async-start(), calls=%async_computation.3 | async-start | bytes 1048576 | tf_op jit(solution)/shard_map/psum | solution.py:34
  253.0 1.4 copy-start.21
  285.5 1.4 copy-start.5
  290.9 111.8 %copy-start.1 = (bf16[8,128,128]{2,1,0:T(8,128)(2,1)S(1)}, bf16[8,128,128]{2,1,0:T(8,128)(2,1)}, u32[]{:S(2)}) copy-start(bf16[8,128,128]{2,1,0:T(8,128)(2,1)} %param.15) | copy-start | bytes 786436
  (10 other events, 10.7 us)
Sparse Core Ops, SparseCore 0:
  15.8 45.9 all-gather.6
  63.7 40.6 all-gather.4
  150.3 131.7 all-gather.8
  291.1 108.8 all-reduce.1
